TPU v7x, 32 devices: a whole 2x2x4 slice. The times are simulated.
32 devices in a mesh: band: 2 (over y), slab: 16 (over z, x, core).
Axes of the slice: x: 2, y: 2, z: 4, core: 2. Of those that a mesh axis runs over, the one named last changes fastest.
Arguments:
- own_orbitals: float32 [4, 128, 128, 128], P('band', 'slab'), may hold values from -6 to 6
- partners: float32 [8, 128, 128, 128], P('band', 'slab'), may hold values from -6 to 6
Outputs:
- own_field: float32 [4, 128, 128, 128], P('band', 'slab')
- partner_field: float32 [8, 128, 128, 128], P('band', 'slab')
All inputs are finite; a program needn't handle non-finite values.
Results may differ from a plain program's by a relative error of at most 0.0001.
Values sent between devices are 32-bit elements; how exact they have to be, the bound alone decides.
No kernel may reach another device: no remote copies, remote signals or barrier semaphores. Data moves between devices by JAX's collectives and lax.ppermute only.
A program may use at most 128 MiB of HBM per device.

v0:
```python
import math
import jax
import jax.numpy as jnp
from jax import lax
from jax.sharding import PartitionSpec as P

STEPS = 2
coulomb_scale = 46.9 * 46.9 / math.pi
highest = lax.Precision.HIGHEST


def passed_along(block, axis, distance):
    devices = range(lax.axis_size(axis))
    route = [((i - distance) % len(devices), i) for i in devices]
    return lax.ppermute(block, axis, route)


def dft_tables(length):
    positions = lax.iota(jnp.int32, length)
    wrapped = positions[:, None] * positions[None, :] % length
    angles = wrapped.astype(jnp.float32) * (2.0 * math.pi / length)
    return (jnp.cos(angles), jnp.sin(angles))


def apply_table(pattern, field, table):
    return jnp.einsum(pattern, field, table, precision=highest)


def forward(pattern, real_part, imag_part, cosine, sine_table):
    new_real = apply_table(pattern, real_part, cosine) + apply_table(pattern, imag_part, sine_table)
    new_imag = apply_table(pattern, imag_part, cosine) - apply_table(pattern, real_part, sine_table)
    return (new_real, new_imag)


def inverse(pattern, real_part, imag_part, cosine, sine_table):
    new_real = apply_table(pattern, real_part, cosine) - apply_table(pattern, imag_part, sine_table)
    new_imag = apply_table(pattern, imag_part, cosine) + apply_table(pattern, real_part, sine_table)
    return (new_real, new_imag)


def frequency(positions, length):
    return jnp.where(positions < length // 2, positions, positions - length).astype(jnp.float32)


def shards(own_orbitals, partners):
    length = own_orbitals.shape[3]
    cosine, sine_table = dft_tables(length)
    slab_count = lax.axis_size("slab")
    rows_y = length // slab_count
    z_waves = frequency(lax.iota(jnp.int32, length), length)
    y_waves = frequency(lax.axis_index("slab") * rows_y + lax.iota(jnp.int32, rows_y), length)
    square = (
        z_waves[:, None, None] * z_waves[:, None, None]
        + y_waves[None, :, None] * y_waves[None, :, None]
        + z_waves[None, None, :] * z_waves[None, None, :]
    )
    kernel = jnp.where(square > 0, coulomb_scale / jnp.maximum(square, 1.0), 0.0) / float(
        length * length * length
    )
    x_form = "pzyx,xk->pzyk"
    y_form = "pzyx,yk->pzkx"
    z_form = "pzyx,zk->pkyx"
    own_acc = jnp.zeros(own_orbitals.shape, jnp.float32)
    partner_set = passed_along(partners, "band", 1)
    partner_out = jnp.zeros(partners.shape, jnp.float32)
    for step_no in range(1, STEPS + 1):
        if step_no > 1:
            partner_set = passed_along(partner_set, "band", 1)
        own_count = own_orbitals.shape[0]
        part_count = partner_set.shape[0]
        pair_count = own_count * part_count
        density = (own_orbitals[:, None] * partner_set[None]).reshape(
            (pair_count,) + own_orbitals.shape[1:]
        )
        potentials_real_part = apply_table(x_form, density, cosine)
        potentials_imag_part = -apply_table(x_form, density, sine_table)
        solve_real_part = potentials_real_part
        solve_imag_part = potentials_imag_part
        solve_real_part, solve_imag_part = forward(
            y_form, solve_real_part, solve_imag_part, cosine, sine_table
        )
        real_part, imag_part = forward(
            z_form,
            lax.all_to_all(solve_real_part, "slab", split_axis=2, concat_axis=1, tiled=True),
            lax.all_to_all(solve_imag_part, "slab", split_axis=2, concat_axis=1, tiled=True),
            cosine,
            sine_table,
        )
        real_part = real_part * kernel
        imag_part = imag_part * kernel
        real_part, imag_part = inverse(z_form, real_part, imag_part, cosine, sine_table)
        solve_real_part = lax.all_to_all(real_part, "slab", split_axis=1, concat_axis=2, tiled=True)
        solve_imag_part = lax.all_to_all(imag_part, "slab", split_axis=1, concat_axis=2, tiled=True)
        potentials_real_part, potentials_imag_part = inverse(
            y_form, solve_real_part, solve_imag_part, cosine, sine_table
        )
        potential = apply_table(x_form, potentials_real_part, cosine) - apply_table(
            x_form, potentials_imag_part, sine_table
        )
        potential = potential.reshape((own_count, part_count) + own_orbitals.shape[1:])
        own_add = jnp.sum(potential * partner_set[None], axis=1)
        part_add = jnp.sum(potential * own_orbitals[:, None], axis=0)
        own_add, part_add = (own_add, part_add)
        own_acc = own_acc + own_add
        partner_out = partner_out + passed_along(part_add, "band", -step_no)
    return (own_acc, partner_out)


def solution(mesh):
    in_specs = (P("band", "slab", None, None), P("band", "slab", None, None))
    out_specs = (P("band", "slab", None, None), P("band", "slab", None, None))
    return jax.shard_map(shards, mesh=mesh, in_specs=in_specs, out_specs=out_specs, check_vma=False)
```

profile of v0, /device:TPU:14, one launch (start us, length us, event | category | flops | bytes accessed | tf_op | source)
XLA Modules:
  0.0 983.0 jit_solution(5613835076587833565)
XLA Ops:
  1.2 47.1 %collective-permute-done = f32[4,8,128,128]{3,2,1,0:T(8,128)S(1)} collective-permute-done((f32[4,8,128,128]{3,2,1,0:T(8,128)}, f32[4,8,128,128]{3,2,1,0:T(8,128)S(1)}, u32[]{:S(2)}, u32[]{:S(2)}) %collective-permute-start) | collective-permute-done | bytes 2097184 | tf_op jit(solution)/shard_map/ppermute | solution.py:15
  48.8 46.0 %collective-permute-done.1 = f32[4,8,128,128]{3,2,1,0:T(8,128)S(1)} collective-permute-done((f32[4,8,128,128]{3,2,1,0:T(8,128)S(1)}, f32[4,8,128,128]{3,2,1,0:T(8,128)S(1)}, u32[]{:S(2)}, u32[]{:S(2)}) %collective-permute-start.1) | collective-permute-done | bytes 2097184 | tf_op jit(solution)/shard_map/ppermute | solution.py:15
  94.8 4.7 broadcast_multiply_fusion
  107.0 4.3 fusion.148
  111.3 3.9 add_bitcast_fusion.1
  115.3 4.4 copy.136
  119.7 6.8 all-to-all-start.4
  126.5 6.1 fusion.125
  132.6 3.9 subtract_bitcast_fusion.1
  136.5 4.4 copy.141
  140.9 77.8 %all-to-all-done.4 = f32[8,8,128,128]{3,1,0,2:T(8,128)} async-done(((f32[8,8,128,128]{3,1,0,2:T(8,128)}), f32[8,8,128,128]{3,1,0,2:T(8,128)}, u32[]{:S(2)}, u32[]{:S(2)}) %all-to-all-start.4) | async-done | bytes 4194336 | tf_op jit(solution)/shard_map/all_to_all | solution.py:84
  218.6 5.0 all-to-all-start.5
  223.7 6.0 fusion.161
  233.4 4.0 fusion.134
  237.5 3.9 subtract_bitcast_fusion.3
  241.4 4.7 copy.115
  246.1 69.9 %all-to-all-done.5 = f32[8,8,128,128]{3,1,0,2:T(8,128)} async-done(((f32[8,8,128,128]{3,1,0,2:T(8,128)}), f32[8,8,128,128]{3,1,0,2:T(8,128)}, u32[]{:S(2)}, u32[]{:S(2)}) %all-to-all-start.5) | async-done | bytes 4194336 | tf_op jit(solution)/shard_map/all_to_all | solution.py:85
  316.0 5.1 all-to-all-start.1
  321.1 6.1 fusion.163
  327.1 3.9 add_bitcast_fusion.3
  331.1 4.4 copy.110
  335.5 77.9 %all-to-all-done.1 = f32[8,8,128,128]{3,1,0,2:T(8,128)} async-done(((f32[8,8,128,128]{3,1,0,2:T(8,128)}), f32[8,8,128,128]{3,1,0,2:T(8,128)}, u32[]{:S(2)}, u32[]{:S(2)}) %all-to-all-start.1) | async-done | bytes 4194336 | tf_op jit(solution)/shard_map/all_to_all | solution.py:85
  413.4 5.6 all-to-all-start
  419.3 5.9 fusion.16
  425.3 6.0 fusion.18
  431.2 6.2 subtract_multiply_fusion
  439.4 4.0 fusion.14
  443.5 6.3 add_multiply_fusion
  449.8 4.1 subtract_bitcast_fusion
  453.9 4.4 copy.148
  458.3 52.8 %all-to-all-done = f32[8,8,128,128]{3,1,0,2:T(8,128)} async-done(((f32[8,8,128,128]{3,1,0,2:T(8,128)}), f32[8,8,128,128]{3,1,0,2:T(8,128)}, u32[]{:S(2)}, u32[]{:S(2)}) %all-to-all-start) | async-done | bytes 4194336 | tf_op jit(solution)/shard_map/all_to_all | solution.py:84
  511.2 5.4 all-to-all-start.6
  516.6 6.1 fusion.12
  522.7 4.1 add_bitcast_fusion
  526.7 4.4 copy.154
  531.1 77.6 %all-to-all-done.6 = f32[8,128,8,128]{3,2,0,1:T(8,128)} async-done(((f32[8,128,8,128]{3,2,0,1:T(8,128)}), f32[8,128,8,128]{3,2,0,1:T(8,128)}, u32[]{:S(2)}, u32[]{:S(2)}) %all-to-all-start.6) | async-done | bytes 4194336 | tf_op jit(solution)/shard_map/all_to_all | solution.py:92
  608.7 5.6 all-to-all-start.7
  614.3 6.0 fusion.46
  620.3 5.9 fusion.44
  626.3 6.2 subtract_multiply_fusion.1
  634.4 4.0 fusion.42
  638.4 6.3 add_multiply_fusion.1
  644.7 4.1 subtract_bitcast_fusion.2
  648.8 4.5 copy.122
  653.3 53.2 %all-to-all-done.7 = f32[8,128,8,128]{3,2,0,1:T(8,128)} async-done(((f32[8,128,8,128]{3,2,0,1:T(8,128)}), f32[8,128,8,128]{3,2,0,1:T(8,128)}, u32[]{:S(2)}, u32[]{:S(2)}) %all-to-all-start.7) | async-done | bytes 4194336 | tf_op jit(solution)/shard_map/all_to_all | solution.py:93
  706.5 5.4 all-to-all-start.2
  711.9 6.1 fusion.40
  718.0 4.1 add_bitcast_fusion.2
  722.1 4.4 copy.128
  726.4 77.6 %all-to-all-done.2 = f32[8,128,8,128]{3,2,0,1:T(8,128)} async-done(((f32[8,128,8,128]{3,2,0,1:T(8,128)}), f32[8,128,8,128]{3,2,0,1:T(8,128)}, u32[]{:S(2)}, u32[]{:S(2)}) %all-to-all-start.2) | async-done | bytes 4194336 | tf_op jit(solution)/shard_map/all_to_all | solution.py:92
  804.1 5.4 all-to-all-start.3
  809.5 8.2 fusion.8
  817.7 8.1 fusion.10
  825.8 8.3 fusion.4
  834.2 8.2 fusion.6
  842.4 8.3 fusion.36
  850.7 8.4 fusion.38
  859.1 42.3 %all-to-all-done.3 = f32[8,128,8,128]{3,2,0,1:T(8,128)} async-done(((f32[8,128,8,128]{3,2,0,1:T(8,128)}), f32[8,128,8,128]{3,2,0,1:T(8,128)}, u32[]{:S(2)}, u32[]{:S(2)}) %all-to-all-start.3) | async-done | bytes 4194336 | tf_op jit(solution)/shard_map/all_to_all | solution.py:93
  901.4 6.0 fusion.32
  907.4 6.1 fusion.34
  913.6 3.8 fusion
  921.3 6.0 multiply_reduce_fusion.2
  927.3 4.4 multiply_reduce_fusion.3
  934.9 46.1 %collective-permute-done.2 = f32[4,8,128,128]{3,2,1,0:T(8,128)S(1)} collective-permute-done((f32[4,8,128,128]{3,2,1,0:T(8,128)S(1)}, f32[4,8,128,128]{3,2,1,0:T(8,128)S(1)}, u32[]{:S(2)}, u32[]{:S(2)}) %collective-permute-start.2) | collective-permute-done | bytes 2097184 | tf_op jit(solution)/shard_map/ppermute | solution.py:15
  (58 shorter events, 25.2 us)
Async XLA Ops:
  0.6 47.6 %collective-permute-start = (f32[4,8,128,128]{3,2,1,0:T(8,128)}, f32[4,8,128,128]{3,2,1,0:T(8,128)S(1)}, u32[]{:S(2)}, u32[]{:S(2)}) collective-permute-start(f32[4,8,128,128]{3,2,1,0:T(8,128)} %param.3), channel_id=1, source_target_pairs={{16,0},{0,16},{17,1},{1,17},{18,2},{2,18},{19,3},{3,19},{20,4},{4,... | collective-permute-start | bytes 6291464 | tf_op jit(solution)/shard_map/ppermute | solution.py:15
  48.3 46.5 %collective-permute-start.1 = (f32[4,8,128,128]{3,2,1,0:T(8,128)S(1)}, f32[4,8,128,128]{3,2,1,0:T(8,128)S(1)}, u32[]{:S(2)}, u32[]{:S(2)}) collective-permute-start(f32[4,8,128,128]{3,2,1,0:T(8,128)S(1)} %collective-permute-done), channel_id=1, source_target_pairs={{16,0},{0,16},{17,1},{1,17},{18,2},{2,18},{19,3},{3,19},{20,4},{4,... | collective-permute-start | bytes 6291464 | tf_op jit(solution)/shard_map/ppermute | solution.py:15
  94.8 4.7 copy-start.19
  103.3 3.7 copy-start.12
  107.0 8.3 copy-start.6
  119.7 99.0 %all-to-all-start.4 = ((f32[8,8,128,128]{3,1,0,2:T(8,128)}), f32[8,8,128,128]{3,1,0,2:T(8,128)}, u32[]{:S(2)}, u32[]{:S(2)}) async-start(f32[8,8,128,128]{3,1,0,2:T(8,128)} %copy.136), calls=%async_computation.4 | async-start | bytes 8388608 | tf_op jit(solution)/shard_map/all_to_all | solution.py:84
  126.5 6.1 copy-start.7
  218.6 97.4 %all-to-all-start.5 = ((f32[8,8,128,128]{3,1,0,2:T(8,128)}), f32[8,8,128,128]{3,1,0,2:T(8,128)}, u32[]{:S(2)}, u32[]{:S(2)}) async-start(f32[8,8,128,128]{3,1,0,2:T(8,128)} %copy.141), calls=%async_computation.5 | async-start | bytes 8388608 | tf_op jit(solution)/shard_map/all_to_all | solution.py:85
  223.7 6.0 copy-start.10
  229.7 3.7 copy-start.11
  233.4 4.1 copy-start.4
  316.0 97.4 %all-to-all-start.1 = ((f32[8,8,128,128]{3,1,0,2:T(8,128)}), f32[8,8,128,128]{3,1,0,2:T(8,128)}, u32[]{:S(2)}, u32[]{:S(2)}) async-start(f32[8,8,128,128]{3,1,0,2:T(8,128)} %copy.115), calls=%async_computation.1 | async-start | bytes 8388608 | tf_op jit(solution)/shard_map/all_to_all | solution.py:85
  321.1 6.1 copy-start.5
  413.4 97.8 %all-to-all-start = ((f32[8,8,128,128]{3,1,0,2:T(8,128)}), f32[8,8,128,128]{3,1,0,2:T(8,128)}, u32[]{:S(2)}, u32[]{:S(2)}) async-start(f32[8,8,128,128]{3,1,0,2:T(8,128)} %copy.110), calls=%async_computation | async-start | bytes 8388608 | tf_op jit(solution)/shard_map/all_to_all | solution.py:84
  437.4 2.0 copy-start.9
  449.8 4.1 copy-start.2
  511.2 97.6 %all-to-all-start.6 = ((f32[8,128,8,128]{3,2,0,1:T(8,128)}), f32[8,128,8,128]{3,2,0,1:T(8,128)}, u32[]{:S(2)}, u32[]{:S(2)}) async-start(f32[8,128,8,128]{3,2,0,1:T(8,128)} %copy.148), calls=%async_computation.6 | async-start | bytes 8388608 | tf_op jit(solution)/shard_map/all_to_all | solution.py:92
  516.6 6.1 copy-start.3
  608.7 97.8 %all-to-all-start.7 = ((f32[8,128,8,128]{3,2,0,1:T(8,128)}), f32[8,128,8,128]{3,2,0,1:T(8,128)}, u32[]{:S(2)}, u32[]{:S(2)}) async-start(f32[8,128,8,128]{3,2,0,1:T(8,128)} %copy.154), calls=%async_computation.7 | async-start | bytes 8388608 | tf_op jit(solution)/shard_map/all_to_all | solution.py:93
  632.4 1.9 copy-start.8
  644.7 4.1 copy-start
  706.5 97.6 %all-to-all-start.2 = ((f32[8,128,8,128]{3,2,0,1:T(8,128)}), f32[8,128,8,128]{3,2,0,1:T(8,128)}, u32[]{:S(2)}, u32[]{:S(2)}) async-start(f32[8,128,8,128]{3,2,0,1:T(8,128)} %copy.122), calls=%async_computation.2 | async-start | bytes 8388608 | tf_op jit(solution)/shard_map/all_to_all | solution.py:92
  711.9 6.1 copy-start.1
  804.1 97.4 %all-to-all-start.3 = ((f32[8,128,8,128]{3,2,0,1:T(8,128)}), f32[8,128,8,128]{3,2,0,1:T(8,128)}, u32[]{:S(2)}, u32[]{:S(2)}) async-start(f32[8,128,8,128]{3,2,0,1:T(8,128)} %copy.128), calls=%async_computation.3 | async-start | bytes 8388608 | tf_op jit(solution)/shard_map/all_to_all | solution.py:93
  907.4 6.2 copy-start.16
  907.4 6.2 copy-start.17
  913.6 3.9 copy-start.18
  917.4 3.9 copy-start.14
  917.4 3.9 copy-start.15
  921.3 6.0 copy-start.13
  927.3 4.4 copy-start.20
  933.1 47.9 %collective-permute-start.2 = (f32[4,8,128,128]{3,2,1,0:T(8,128)S(1)}, f32[4,8,128,128]{3,2,1,0:T(8,128)S(1)}, u32[]{:S(2)}, u32[]{:S(2)}) collective-permute-start(f32[4,8,128,128]{3,2,1,0:T(8,128)S(1)} %get-tuple-element.3), channel_id=1, source_target_pairs={{16,0},{0,16},{17,1},{1,17},{18,2},{2,18},{19,3},{3,19},{20,4},{4,... | collective-permute-start | bytes 6291464 | tf_op jit(solution)/shard_map/ppermute | solution.py:15
  933.7 47.3 %collective-permute-start.3 = (f32[4,8,128,128]{3,2,1,0:T(8,128)S(1)}, f32[4,8,128,128]{3,2,1,0:T(8,128)S(1)}, u32[]{:S(2)}, u32[]{:S(2)}) collective-permute-start(f32[4,8,128,128]{3,2,1,0:T(8,128)S(1)} %get-tuple-element.2), channel_id=1, source_target_pairs={{0,0},{16,16},{1,1},{17,17},{2,2},{18,18},{3,3},{19,19},{4,4},{20,... | collective-permute-start | bytes 6291464 | tf_op jit(solution)/shard_map/ppermute | solution.py:15
where the time goes:
time: 992 us; the launch traced here: 983 us
  waiting for transfers between devices  668 us (67%)
  matrix products  218 us (22%)
  starting transfers between devices  46.1 us (5%)
  local copies, waits for them, and re-layouts  39.5 us (4%)
    dot_general x40, matrix products, apply_table(): return jnp.einsum(pattern, field, table, precision=highest)  218 us
    all_to_all x2, waiting for transfers between devices, shards(): lax.all_to_all(real_part, 'slab', split_axis=1, concat_axis=2, tiled=True)  155 us
    all_to_all x2, waiting for transfers between devices, shards(): lax.all_to_all(solve_imag_part, 'slab', split_axis=2, concat_axis=1, tile...  148 us
    ppermute x4, waiting for transfers between devices, passed_along(): return lax.ppermute(block, axis, route)  139 us
    all_to_all x2, waiting for transfers between devices, shards(): lax.all_to_all(solve_real_part, 'slab', split_axis=2, concat_axis=1, tile...  131 us
    all_to_all x2, waiting for transfers between devices, shards(): lax.all_to_all(imag_part, 'slab', split_axis=1, concat_axis=2, tiled=True)  95.5 us
  transfers between devices with their start and end apart: 12, of which 11 were waited for; matrix products, arithmetic and copies ran while one was open for 21% of the time, Pallas kernels for 0%

commit v1 on v0

--- a/solution.py
+++ b/solution.py
@@ -7,6 +7,13 @@
 STEPS = 2
 coulomb_scale = 46.9 * 46.9 / math.pi
 highest = lax.Precision.HIGHEST
+
+
+def swap_blocks(shard, axis, split, join):
+    count = lax.axis_size(axis)
+    tiles = jnp.stack(jnp.split(shard, count, axis=split), axis=0)
+    tiles = lax.all_to_all(tiles, axis, split_axis=0, concat_axis=0)
+    return jnp.concatenate(tiles, axis=join)
 
 
 def passed_along(block, axis, distance):
@@ -82,7 +89,7 @@
         real_part, imag_part = forward(
             z_form,
             lax.all_to_all(solve_real_part, "slab", split_axis=2, concat_axis=1, tiled=True),
-            lax.all_to_all(solve_imag_part, "slab", split_axis=2, concat_axis=1, tiled=True),
+            swap_blocks(solve_imag_part, "slab", 2, 1),
             cosine,
             sine_table,
         )

time: 992 us -> 997 us (level)
  local copies, waits for them, and re-layouts: 39.5 us -> 59.9 us
    unnamed x42 -> x76, local copies, waits for them, and re-layouts: 4.03 us -> 26.6 us
    all_to_all x2, waiting for transfers between devices: 131 us -> 115 us  [shards(): lax.all_to_all(solve_real_part, 'slab', split_axis=2, concat_axis=1, tile...]
  transfers between devices with their start and end apart: 12 -> 12, of which waited for: 11 -> 11; matrix products, arithmetic and copies ran while one was open for 21% -> 22% of each run, Pallas kernels for 0% -> 0%
where the time goes in v1:
time: 997 us; the launch traced here: 987 us
  waiting for transfers between devices  660 us (66%)
  matrix products  213 us (21%)
  local copies, waits for them, and re-layouts  59.9 us (6%)
  starting transfers between devices  44.2 us (4%)
    dot_general x40, matrix products, apply_table(): return jnp.einsum(pattern, field, table, precision=highest)  213 us
    all_to_all x2, waiting for transfers between devices, swap_blocks(): tiles = lax.all_to_all(tiles, axis, split_axis=0, concat_axis=0)  156 us
    all_to_all x2, waiting for transfers between devices, shards(): lax.all_to_all(real_part, 'slab', split_axis=1, concat_axis=2, tiled=True)  155 us
    ppermute x4, waiting for transfers between devices, passed_along(): return lax.ppermute(block, axis, route)  139 us
    all_to_all x2, waiting for transfers between devices, shards(): lax.all_to_all(solve_real_part, 'slab', split_axis=2, concat_axis=1, tile...  115 us
    all_to_all x2, waiting for transfers between devices, shards(): lax.all_to_all(imag_part, 'slab', split_axis=1, concat_axis=2, tiled=True)  95.3 us
    unnamed x76, local copies, waits for them, and re-layouts  26.6 us
  transfers between devices with their start and end apart: 12, of which 11 were waited for; matrix products, arithmetic and copies ran while one was open for 22% of the time, Pallas kernels for 0%

profile of v1, /device:TPU:14, one launch (start us, length us, event | category | flops | bytes accessed | tf_op | source)
XLA Modules:
  0.0 987.4 jit_solution(18206243054293118948)
XLA Ops:
  1.2 47.1 %collective-permute-done = f32[4,8,128,128]{3,2,1,0:T(8,128)S(1)} collective-permute-done((f32[4,8,128,128]{3,2,1,0:T(8,128)}, f32[4,8,128,128]{3,2,1,0:T(8,128)S(1)}, u32[]{:S(2)}, u32[]{:S(2)}) %collective-permute-start) | collective-permute-done | bytes 2097184 | tf_op jit(solution)/shard_map/ppermute | solution.py:22
  48.8 46.0 %collective-permute-done.1 = f32[4,8,128,128]{3,2,1,0:T(8,128)S(1)} collective-permute-done((f32[4,8,128,128]{3,2,1,0:T(8,128)S(1)}, f32[4,8,128,128]{3,2,1,0:T(8,128)S(1)}, u32[]{:S(2)}, u32[]{:S(2)}) %collective-permute-start.1) | collective-permute-done | bytes 2097184 | tf_op jit(solution)/shard_map/ppermute | solution.py:22
  94.8 4.0 broadcast_multiply_fusion
  98.7 3.8 fusion.186
  106.3 4.3 fusion.153
  110.6 3.9 subtract_bitcast_fusion.1
  126.4 6.2 all-to-all-start.5
  132.6 6.1 fusion.176
  138.7 3.9 add_bitcast_fusion.1
  142.6 4.4 copy.141
  147.0 77.9 %all-to-all-done.5 = f32[16,8,8,8,128]{4,3,2,1,0:T(8,128)} async-done(((f32[16,8,8,8,128]{4,3,2,1,0:T(8,128)}), f32[16,8,8,8,128]{4,3,2,1,0:T(8,128)}, u32[]{:S(2)}, u32[]{:S(2)}) %all-to-all-start.5) | async-done | bytes 4194336 | tf_op jit(solution)/shard_map/all_to_all | solution.py:15
  224.9 5.1 all-to-all-start.4
  230.0 6.3 fusion.189
  240.0 4.0 fusion.162
  244.0 3.9 subtract_bitcast_fusion.3
  260.1 62.2 %all-to-all-done.4 = f32[8,8,128,128]{3,1,0,2:T(8,128)} async-done(((f32[8,8,128,128]{3,1,0,2:T(8,128)}), f32[8,8,128,128]{3,1,0,2:T(8,128)}, u32[]{:S(2)}, u32[]{:S(2)}) %all-to-all-start.4) | async-done | bytes 4194336 | tf_op jit(solution)/shard_map/all_to_all | solution.py:91
  322.3 5.1 all-to-all-start.1
  327.4 6.1 fusion.191
  333.4 3.9 add_bitcast_fusion.3
  337.4 4.4 copy.114
  341.8 77.9 %all-to-all-done.1 = f32[16,8,8,8,128]{4,3,2,1,0:T(8,128)} async-done(((f32[16,8,8,8,128]{4,3,2,1,0:T(8,128)}), f32[16,8,8,8,128]{4,3,2,1,0:T(8,128)}, u32[]{:S(2)}, u32[]{:S(2)}) %all-to-all-start.1) | async-done | bytes 4194336 | tf_op jit(solution)/shard_map/all_to_all | solution.py:15
  419.7 5.1 all-to-all-start
  427.8 6.0 fusion.18
  433.8 6.2 fusion.16
  440.0 4.7 subtract_multiply_fusion
  446.7 4.0 fusion.14
  450.8 5.1 add_multiply_fusion
  455.9 4.1 subtract_bitcast_fusion
  460.0 4.4 copy.154
  464.4 52.6 %all-to-all-done = f32[8,8,128,128]{3,1,0,2:T(8,128)} async-done(((f32[8,8,128,128]{3,1,0,2:T(8,128)}), f32[8,8,128,128]{3,1,0,2:T(8,128)}, u32[]{:S(2)}, u32[]{:S(2)}) %all-to-all-start) | async-done | bytes 4194336 | tf_op jit(solution)/shard_map/all_to_all | solution.py:91
  517.0 5.4 all-to-all-start.6
  522.4 6.1 fusion.12
  528.5 4.1 add_bitcast_fusion
  532.6 4.4 copy.160
  537.0 77.6 %all-to-all-done.6 = f32[8,128,8,128]{3,2,0,1:T(8,128)} async-done(((f32[8,128,8,128]{3,2,0,1:T(8,128)}), f32[8,128,8,128]{3,2,0,1:T(8,128)}, u32[]{:S(2)}, u32[]{:S(2)}) %all-to-all-start.6) | async-done | bytes 4194336 | tf_op jit(solution)/shard_map/all_to_all | solution.py:99
  614.6 5.0 all-to-all-start.7
  622.4 6.0 fusion.42
  628.4 6.2 fusion.40
  634.5 4.7 subtract_multiply_fusion.1
  641.3 4.0 fusion.38
  645.3 5.1 add_multiply_fusion.1
  650.5 4.1 subtract_bitcast_fusion.2
  654.5 4.4 copy.127
  658.9 53.1 %all-to-all-done.7 = f32[8,128,8,128]{3,2,0,1:T(8,128)} async-done(((f32[8,128,8,128]{3,2,0,1:T(8,128)}), f32[8,128,8,128]{3,2,0,1:T(8,128)}, u32[]{:S(2)}, u32[]{:S(2)}) %all-to-all-start.7) | async-done | bytes 4194336 | tf_op jit(solution)/shard_map/all_to_all | solution.py:100
  712.0 5.4 all-to-all-start.2
  717.3 6.1 fusion.36
  723.4 4.1 add_bitcast_fusion.2
  727.5 4.4 copy.133
  731.9 77.6 %all-to-all-done.2 = f32[8,128,8,128]{3,2,0,1:T(8,128)} async-done(((f32[8,128,8,128]{3,2,0,1:T(8,128)}), f32[8,128,8,128]{3,2,0,1:T(8,128)}, u32[]{:S(2)}, u32[]{:S(2)}) %all-to-all-start.2) | async-done | bytes 4194336 | tf_op jit(solution)/shard_map/all_to_all | solution.py:99
  809.5 5.2 all-to-all-start.3
  814.7 8.2 fusion.8
  823.0 8.1 fusion.10
  831.1 8.6 fusion.4
  839.7 8.2 fusion.6
  847.9 8.3 fusion.32
  856.1 8.4 fusion.34
  864.6 42.3 %all-to-all-done.3 = f32[8,128,8,128]{3,2,0,1:T(8,128)} async-done(((f32[8,128,8,128]{3,2,0,1:T(8,128)}), f32[8,128,8,128]{3,2,0,1:T(8,128)}, u32[]{:S(2)}, u32[]{:S(2)}) %all-to-all-start.3) | async-done | bytes 4194336 | tf_op jit(solution)/shard_map/all_to_all | solution.py:100
  906.9 6.0 fusion.28
  912.9 6.1 fusion.30
  919.0 3.8 fusion
  922.9 3.8 fusion.24
  926.8 5.0 multiply_reduce_fusion.2
  931.8 4.3 multiply_reduce_fusion.3
  939.4 46.1 %collective-permute-done.2 = f32[4,8,128,128]{3,2,1,0:T(8,128)S(1)} collective-permute-done((f32[4,8,128,128]{3,2,1,0:T(8,128)S(1)}, f32[4,8,128,128]{3,2,1,0:T(8,128)S(1)}, u32[]{:S(2)}, u32[]{:S(2)}) %collective-permute-start.2) | collective-permute-done | bytes 2097184 | tf_op jit(solution)/shard_map/ppermute | solution.py:22
  (94 shorter events, 47.2 us)
Async XLA Ops:
  0.6 47.6 %collective-permute-start = (f32[4,8,128,128]{3,2,1,0:T(8,128)}, f32[4,8,128,128]{3,2,1,0:T(8,128)S(1)}, u32[]{:S(2)}, u32[]{:S(2)}) collective-permute-start(f32[4,8,128,128]{3,2,1,0:T(8,128)} %param.3), channel_id=1, source_target_pairs={{16,0},{0,16},{17,1},{1,17},{18,2},{2,18},{19,3},{3,19},{20,4},{4,... | collective-permute-start | bytes 6291464 | tf_op jit(solution)/shard_map/ppermute | solution.py:22
  48.3 50.5 %copy-start.19 = (f32[4,8,128,128]{3,2,1,0:T(8,128)}, f32[4,8,128,128]{3,2,1,0:T(8,128)S(1)}, u32[]{:S(2)}) copy-start(f32[4,8,128,128]{3,2,1,0:T(8,128)S(1)} %collective-permute-done) | copy-start | bytes 6291460
  48.3 46.5 %collective-permute-start.1 = (f32[4,8,128,128]{3,2,1,0:T(8,128)S(1)}, f32[4,8,128,128]{3,2,1,0:T(8,128)S(1)}, u32[]{:S(2)}, u32[]{:S(2)}) collective-permute-start(f32[4,8,128,128]{3,2,1,0:T(8,128)S(1)} %collective-permute-done), channel_id=1, source_target_pairs={{16,0},{0,16},{17,1},{1,17},{18,2},{2,18},{19,3},{3,19},{20,4},{4,... | collective-permute-start | bytes 6291464 | tf_op jit(solution)/shard_map/ppermute | solution.py:22
  102.6 3.7 copy-start.12
  106.3 8.2 copy-start.6
  126.4 98.6 %all-to-all-start.5 = ((f32[16,8,8,8,128]{4,3,2,1,0:T(8,128)}), f32[16,8,8,8,128]{4,3,2,1,0:T(8,128)}, u32[]{:S(2)}, u32[]{:S(2)}) async-start(f32[16,8,8,8,128]{4,3,2,1,0:T(8,128)} %fusion.113), calls=%async_computation.5 | async-start | bytes 8388608 | tf_op jit(solution)/shard_map/all_to_all | solution.py:15
  132.6 6.1 copy-start.7
  224.9 97.4 %all-to-all-start.4 = ((f32[8,8,128,128]{3,1,0,2:T(8,128)}), f32[8,8,128,128]{3,1,0,2:T(8,128)}, u32[]{:S(2)}, u32[]{:S(2)}) async-start(f32[8,8,128,128]{3,1,0,2:T(8,128)} %copy.141), calls=%async_computation.4 | async-start | bytes 8388608 | tf_op jit(solution)/shard_map/all_to_all | solution.py:91
  230.0 6.3 copy-start.10
  236.3 3.7 copy-start.11
  240.0 4.1 copy-start.4
  322.3 97.4 %all-to-all-start.1 = ((f32[16,8,8,8,128]{4,3,2,1,0:T(8,128)}), f32[16,8,8,8,128]{4,3,2,1,0:T(8,128)}, u32[]{:S(2)}, u32[]{:S(2)}) async-start(f32[16,8,8,8,128]{4,3,2,1,0:T(8,128)} %fusion.129), calls=%async_computation.1 | async-start | bytes 8388608 | tf_op jit(solution)/shard_map/all_to_all | solution.py:15
  327.4 6.1 copy-start.5
  419.7 97.4 %all-to-all-start = ((f32[8,8,128,128]{3,1,0,2:T(8,128)}), f32[8,8,128,128]{3,1,0,2:T(8,128)}, u32[]{:S(2)}, u32[]{:S(2)}) async-start(f32[8,8,128,128]{3,1,0,2:T(8,128)} %copy.114), calls=%async_computation | async-start | bytes 8388608 | tf_op jit(solution)/shard_map/all_to_all | solution.py:91
  444.7 2.0 copy-start.9
  455.9 4.1 copy-start.2
  517.0 97.5 %all-to-all-start.6 = ((f32[8,128,8,128]{3,2,0,1:T(8,128)}), f32[8,128,8,128]{3,2,0,1:T(8,128)}, u32[]{:S(2)}, u32[]{:S(2)}) async-start(f32[8,128,8,128]{3,2,0,1:T(8,128)} %copy.154), calls=%async_computation.6 | async-start | bytes 8388608 | tf_op jit(solution)/shard_map/all_to_all | solution.py:99
  522.4 6.1 copy-start.3
  614.6 97.4 %all-to-all-start.7 = ((f32[8,128,8,128]{3,2,0,1:T(8,128)}), f32[8,128,8,128]{3,2,0,1:T(8,128)}, u32[]{:S(2)}, u32[]{:S(2)}) async-start(f32[8,128,8,128]{3,2,0,1:T(8,128)} %copy.160), calls=%async_computation.7 | async-start | bytes 8388608 | tf_op jit(solution)/shard_map/all_to_all | solution.py:100
  639.3 2.0 copy-start.8
  650.5 4.1 copy-start
  712.0 97.5 %all-to-all-start.2 = ((f32[8,128,8,128]{3,2,0,1:T(8,128)}), f32[8,128,8,128]{3,2,0,1:T(8,128)}, u32[]{:S(2)}, u32[]{:S(2)}) async-start(f32[8,128,8,128]{3,2,0,1:T(8,128)} %copy.127), calls=%async_computation.2 | async-start | bytes 8388608 | tf_op jit(solution)/shard_map/all_to_all | solution.py:99
  717.3 6.1 copy-start.1
  809.5 97.4 %all-to-all-start.3 = ((f32[8,128,8,128]{3,2,0,1:T(8,128)}), f32[8,128,8,128]{3,2,0,1:T(8,128)}, u32[]{:S(2)}, u32[]{:S(2)}) async-start(f32[8,128,8,128]{3,2,0,1:T(8,128)} %copy.133), calls=%async_computation.3 | async-start | bytes 8388608 | tf_op jit(solution)/shard_map/all_to_all | solution.py:100
  912.8 6.2 copy-start.16
  912.8 6.2 copy-start.17
  919.0 3.9 copy-start.18
  922.9 3.9 copy-start.14
  922.9 3.9 copy-start.15
  926.8 5.0 copy-start.13
  926.8 5.0 copy-start.20
  931.8 4.3 copy-start.22
  936.1 2.2 copy-start.21
  937.6 47.9 %collective-permute-start.2 = (f32[4,8,128,128]{3,2,1,0:T(8,128)S(1)}, f32[4,8,128,128]{3,2,1,0:T(8,128)S(1)}, u32[]{:S(2)}, u32[]{:S(2)}) collective-permute-start(f32[4,8,128,128]{3,2,1,0:T(8,128)S(1)} %get-tuple-element.3), channel_id=1, source_target_pairs={{16,0},{0,16},{17,1},{1,17},{18,2},{2,18},{19,3},{3,19},{20,4},{4,... | collective-permute-start | bytes 6291464 | tf_op jit(solution)/shard_map/ppermute | solution.py:22
  938.2 47.3 %collective-permute-start.3 = (f32[4,8,128,128]{3,2,1,0:T(8,128)S(1)}, f32[4,8,128,128]{3,2,1,0:T(8,128)S(1)}, u32[]{:S(2)}, u32[]{:S(2)}) collective-permute-start(f32[4,8,128,128]{3,2,1,0:T(8,128)S(1)} %get-tuple-element.2), channel_id=1, source_target_pairs={{0,0},{16,16},{1,1},{17,17},{2,2},{18,18},{3,3},{19,19},{4,4},{20,... | collective-permute-start | bytes 6291464 | tf_op jit(solution)/shard_map/ppermute | solution.py:22
